TPU v7x, 256 devices: a whole 4x4x8 slice. The times are simulated.
256 devices in a mesh: pipe: 8 (over x, z_hi), expert: 32 (over y, z_lo, core).
Axes of the slice: x: 4, y: 4, z: 8 (z_hi: 2, z_lo: 4; z = z_hi * 4 + z_lo), core: 2. Of those that a mesh axis runs over, the one named last changes fastest.
Arguments:
- fwd_acts: bfloat16 [8, 2048, 3584], P('pipe', 'expert'), may hold values from -6 to 6
- fwd_routes: int32 [8, 2048, 2], P('pipe', 'expert'), may hold values from 0 to 7, all different within a row; in each aligned block of 64 rows (0 to 63, 64 to 127, ..., all dimensions but the last counted through in order) at most 20 rows name the same one
- fwd_gates: float32 [8, 2048, 2], P('pipe', 'expert'), may hold values from 0.25 to 1
- back_acts: bfloat16 [8, 2048, 3584], P('pipe', 'expert'), may hold values from -6 to 6
- back_routes: int32 [8, 2048, 2], P('pipe', 'expert'), may hold values from 0 to 7, all different within a row; in each aligned block of 64 rows (0 to 63, 64 to 127, ..., all dimensions but the last counted through in order) at most 20 rows name the same one
- back_gates: float32 [8, 2048, 2], P('pipe', 'expert'), may hold values from 0.25 to 1
- back_grads: bfloat16 [8, 2048, 3584], P('pipe', 'expert'), may hold values from -0.59765625 to 0.59765625
- w_up: bfloat16 [8, 32, 3584, 256], P('pipe', 'expert'), may hold values from -0.09375 to 0.09375
- w_down: bfloat16 [8, 32, 256, 3584], P('pipe', 'expert'), may hold values from -0.1875 to 0.1875
Outputs:
- fwd_next: bfloat16 [8, 2048, 3584], P('pipe', 'expert')
- back_next: bfloat16 [8, 2048, 3584], P('pipe', 'expert')
- grad_up: float32 [8, 32, 3584, 256], P('pipe', 'expert')
- grad_down: float32 [8, 32, 256, 3584], P('pipe', 'expert')
Inputs may be any that keep to these rules, and one draw needn't show every extreme that they name: `fwd_routes`: in each aligned block of 64 rows of a section the 2 experts of a row differ, and each expert is named by at most 20 rows, by exactly 20 in some block. `back_routes`: as for fwd_routes.
All inputs are finite; a program needn't handle non-finite values.
Results may differ from a plain program's by a relative error of at most 0.005.
Values may be sent and summed in bfloat16 or wider, within the bound.
A program may use at most 192 MiB of HBM per device.

v0:
```python
import jax
import jax.numpy as jnp
from jax import lax
from jax.sharding import PartitionSpec as P

GROUP = 4
HIGH = lax.Precision.HIGHEST


def passed_along(value, axis, steps):
    count = lax.axis_size(axis)
    pairs = [(source, (source + steps) % count) for source in range(count)]
    return lax.ppermute(value, axis, pairs)


def silu_grad(value):
    sigma = jax.nn.sigmoid(value)
    return sigma * (1.0 + value * (1.0 - sigma))


def tables(routes, gates, experts, slot_cap):
    tok_rows, top_count = routes.shape
    flat = routes.reshape(tok_rows * top_count)
    onehot = (flat[:, None] == jnp.arange(experts, dtype=jnp.int32)[None, :]).astype(jnp.int32)
    before = jnp.cumsum(onehot, axis=0) - onehot
    slots = jnp.sum(before * onehot, axis=1)
    places = flat * slot_cap + slots
    columns = jnp.arange(experts * slot_cap, dtype=jnp.int32)
    hits = (
        (places[:, None] == columns[None, :])
        .astype(jnp.float32)
        .reshape(tok_rows, top_count, experts * slot_cap)
    )
    plain = jnp.sum(hits, axis=1)
    gated = jnp.sum(hits * gates[:, :, None], axis=1)
    return (plain, gated)


def gather_rows(plain, values):
    return lax.dot_general(
        plain.astype(jnp.bfloat16),
        values,
        (((0,), (0,)), ((), ())),
        preferred_element_type=jnp.float32,
    ).astype(jnp.bfloat16)


def send_rows(stacked, experts, slot_cap):
    count, _, model_width = stacked.shape
    chunks = stacked.reshape(count, experts, slot_cap, model_width)
    received = lax.all_to_all(chunks, "eg", split_axis=1, concat_axis=1, tiled=True)
    gathered = lax.all_gather(received, "em", axis=1, tiled=True)
    return gathered.reshape(count, -1, model_width)


def send_back(parts, experts, slot_cap):
    count, _, model_width = parts.shape
    arranged = parts.reshape(count, GROUP, experts * slot_cap, model_width)
    received = lax.all_to_all(arranged, "em", split_axis=1, concat_axis=1, tiled=True)
    summed = jnp.sum(received, axis=1, dtype=jnp.float32).astype(jnp.bfloat16)
    summed = summed.reshape(count, experts, slot_cap, model_width)
    back = lax.all_to_all(summed, "eg", split_axis=1, concat_axis=1, tiled=True)
    return back.reshape(count, experts * slot_cap, model_width).astype(jnp.float32)


def expert_forward(rows, up_proj, down_proj):
    pre = jnp.dot(rows, up_proj, preferred_element_type=jnp.float32)
    act = jax.nn.silu(pre).astype(jnp.bfloat16)
    return jnp.dot(act, down_proj, preferred_element_type=jnp.float32).astype(jnp.bfloat16)


def expert_backward(rows, grad_rows, up_proj, down_proj):
    pre = jnp.dot(rows, up_proj, preferred_element_type=jnp.float32)
    act = jax.nn.silu(pre).astype(jnp.bfloat16)
    dact = lax.dot_general(
        grad_rows, down_proj, (((1,), (1,)), ((), ())), preferred_element_type=jnp.float32
    )
    dpre = (dact * silu_grad(pre)).astype(jnp.bfloat16)
    dpart = lax.dot_general(
        dpre, up_proj, (((1,), (1,)), ((), ())), preferred_element_type=jnp.float32
    ).astype(jnp.bfloat16)
    grad_up = lax.dot_general(
        rows, dpre, (((0,), (0,)), ((), ())), preferred_element_type=jnp.float32
    )
    grad_down = lax.dot_general(
        act, grad_rows, (((0,), (0,)), ((), ())), preferred_element_type=jnp.float32
    )
    return (dpart, grad_up, grad_down)


def local(
    fwd_acts, fwd_routes, fwd_gates, back_acts, back_routes, back_gates, back_grads, w_up, w_down
):
    devices = lax.axis_size("eg") * lax.axis_size("em")
    experts = devices // GROUP
    tok_rows = fwd_acts.shape[1]
    top_count = fwd_routes.shape[2]
    slot_cap = GROUP * (5 * tok_rows * top_count // (4 * devices))
    up_proj = w_up[0, 0]
    down_proj = w_down[0, 0]
    fwd_input = fwd_acts[0]
    back_input = back_acts[0]
    out_grad = back_grads[0]
    plain_f, gated_f = tables(fwd_routes[0], fwd_gates[0], experts, slot_cap)
    plain_b, gated_b = tables(back_routes[0], back_gates[0], experts, slot_cap)
    buffer_f = gather_rows(plain_f, fwd_input)
    buffer_x = gather_rows(plain_b, back_input)
    buffer_g = lax.dot_general(
        gated_b, out_grad.astype(jnp.float32), (((0,), (0,)), ((), ())), precision=HIGH
    ).astype(jnp.bfloat16)
    got_f = send_rows(buffer_f[None], experts, slot_cap)
    part = expert_forward(got_f[0], up_proj, down_proj)
    summed_f = send_back(part[None], experts, slot_cap)[0]
    got_b = send_rows(jnp.stack([buffer_x, buffer_g]), experts, slot_cap)
    dpart, grad_up, grad_down = expert_backward(got_b[0], got_b[1], up_proj, down_proj)
    summed_b = send_back(dpart[None], experts, slot_cap)[0]
    merged = jnp.dot(gated_f, summed_f, precision=HIGH)
    section_out = (fwd_input.astype(jnp.float32) + merged).astype(jnp.bfloat16)
    spread_back = jnp.dot(plain_b, summed_b, precision=HIGH)
    section_grad = (out_grad.astype(jnp.float32) + spread_back).astype(jnp.bfloat16)
    fwd_next = passed_along(section_out[None], "pipe", 1)
    back_next = passed_along(section_grad[None], "pipe", -1)
    return (fwd_next, back_next, grad_up[None, None], grad_down[None, None])


def solution(mesh):
    groups = mesh.shape["expert"] // GROUP
    devices = mesh.devices.reshape(mesh.shape["pipe"], groups, GROUP)
    mesh = jax.sharding.Mesh(devices, ("pipe", "eg", "em"))
    in_specs = (
        P("pipe", ("eg", "em"), None),
        P("pipe", ("eg", "em"), None),
        P("pipe", ("eg", "em"), None),
        P("pipe", ("eg", "em"), None),
        P("pipe", ("eg", "em"), None),
        P("pipe", ("eg", "em"), None),
        P("pipe", ("eg", "em"), None),
        P("pipe", ("eg", "em"), None, None),
        P("pipe", ("eg", "em"), None, None),
    )
    out_specs = (
        P("pipe", ("eg", "em"), None),
        P("pipe", ("eg", "em"), None),
        P("pipe", ("eg", "em"), None, None),
        P("pipe", ("eg", "em"), None, None),
    )
    return jax.shard_map(local, mesh=mesh, in_specs=in_specs, out_specs=out_specs, check_vma=False)
```

profile of v0, /device:TPU:1, one launch (start us, length us, event | category | flops | bytes accessed | tf_op | source)
XLA Modules:
  0.0 540.3 jit_solution(244298509199671782)
XLA Ops:
  7.2 0.9 copy.61
  8.1 0.1 eq.58
  8.3 0.1 fusion.28
  8.4 0.2 reduce_window_sum.17
  8.5 0.2 select_reduce_fusion.3
  8.7 0.1 reduce_sum.83
  8.9 0.1 copy.62
  8.9 0.7 bitcast_add_fusion.1
  9.6 1.4 convert_reduce_fusion.1
  11.0 2.5 convolution_convert_fusion.4
  13.5 1.4 reshape_broadcast_in_dim.9
  14.9 41.2 %all_to_all.30 = bf16[1,8,20,3584]{3,2,0,1:T(8,128)(2,1)S(1)} all-to-all(bf16[1,8,20,3584]{3,2,0,1:T(8,128)(2,1)S(1)} %bitcast.73), channel_id=1, replica_groups=mesh['pipe'=8,'eg'=8,'em'=4] {'eg'}, dimensions={1} | all-to-all | bytes 2293760 | tf_op jit(solution)/shard_map/all_to_all | solution.py:51
  56.1 1.3 copy.64
  57.5 0.1 copy.68
  57.6 0.1 eq.65
  57.7 0.1 fusion.27
  57.8 0.2 reduce_window_sum.18
  58.0 0.2 select_reduce_fusion.2
  58.2 0.1 reduce_sum.88
  58.3 0.1 copy.69
  58.4 0.1 select_reduce_fusion
  58.6 0.6 copy-done.5
  59.2 1.5 convolution_convert_fusion.3
  60.6 1.4 stack.9
  62.0 3.1 convolution_convert_fusion.2
  65.1 2.3 stack.10
  67.4 1.7 pad_maximum_fusion
  69.1 2.4 copy.70
  71.4 52.3 %all_to_all.31 = bf16[2,8,20,3584]{3,0,2,1:T(2,128)(2,1)} all-to-all(bf16[2,8,20,3584]{3,0,2,1:T(2,128)(2,1)S(1)} %copy.70), channel_id=1, replica_groups=mesh['pipe'=8,'eg'=8,'em'=4] {'eg'}, dimensions={1} | all-to-all | bytes 4587520 | tf_op jit(solution)/shard_map/all_to_all | solution.py:51
  123.7 12.2 %all-gather.3.cloned.1.call-done = bf16[1,32,20,3584]{3,1,2,0:T(8,128)(2,1)} async-done(((bf16[1,8,20,3584]{3,1,2,0:T(8,128)(2,1)}), bf16[1,32,20,3584]{3,1,2,0:T(8,128)(2,1)}) %all-gather.3.cloned.1.call-update) | async-done | bytes 4587536 | tf_op jit(solution)/shard_map/all_gather | solution.py:52
  135.9 7.3 %copy.65 = bf16[1,32,20,3584]{3,2,1,0:T(8,128)(2,1)} copy(bf16[1,32,20,3584]{3,1,2,0:T(8,128)(2,1)} %all-gather.3.cloned.1.call-done) | data formatting | bytes 9175040 | tf_op jit(solution)/shard_map/all_gather | solution.py:52
  143.2 7.4 %squeeze_reshape.3 = bf16[640,3584]{1,0:T(8,128)(2,1)} reshape(bf16[1,32,20,3584]{3,2,1,0:T(8,128)(2,1)} %copy.65) | data formatting | bytes 9175040 | tf_op jit(solution)/shard_map/squeeze;reshape | solution.py:112
  150.6 10.6 %convolution_convert_fusion.1 = bf16[640,3584]{1,0:T(8,128)(2,1)} fusion(bf16[1,1,256,3584]{3,2,1,0:T(8,128)(2,1)} %param.17, bf16[640,3584]{1,0:T(8,128)(2,1)} %squeeze_reshape.3, bf16[1,1,3584,256]{3,2,1,0:T(8,128)(2,1)S(1)} %copy-done), kind=kOutput, calls=%fused_computation.3 | convolution fusion | flops 2351923200 | bytes 12845056 | tf_op jit(solution)/shard_map/dot_general | solution.py:69
  161.2 5.2 all-to-all-start.1
  166.5 111.3 %all-gather.5.cloned.1.call-done = bf16[2,32,20,3584]{3,0,2,1:T(2,128)(2,1)} async-done(((bf16[2,8,20,3584]{3,0,2,1:T(2,128)(2,1)}), bf16[2,32,20,3584]{3,0,2,1:T(2,128)(2,1)}) %all-gather.5.cloned.1.call-update) | async-done | bytes 9175056 | tf_op jit(solution)/shard_map/all_gather | solution.py:52
  277.7 45.6 %slice_reduce_fusion = (bf16[32,20,3584]{2,1,0:T(8,128)(2,1)}, bf16[32,20,3584]{2,1,0:T(8,128)(2,1)}) fusion(bf16[2,32,20,3584]{3,0,2,1:T(2,128)(2,1)} %all-gather.5.cloned.1.call-done), kind=kLoop, calls=%fused_computation | loop fusion | bytes 18350080 | tf_op jit(solution)/shard_map/slice | solution.py:115
  323.3 7.3 %squeeze.34 = bf16[640,3584]{1,0:T(8,128)(2,1)} reshape(bf16[32,20,3584]{2,1,0:T(8,128)(2,1)} %get-tuple-element.4) | data formatting | bytes 9175040 | tf_op jit(solution)/shard_map/squeeze | solution.py:115
  330.6 7.3 %squeeze.33 = bf16[640,3584]{1,0:T(8,128)(2,1)} reshape(bf16[32,20,3584]{2,1,0:T(8,128)(2,1)} %get-tuple-element.5) | data formatting | bytes 9175040 | tf_op jit(solution)/shard_map/squeeze | solution.py:115
  337.9 3.8 fusion.8
  341.7 0.8 copy-done.3
  342.5 1.4 fusion.15
  343.9 3.6 convolution_convert_fusion
  347.5 4.9 all-to-all-start.4
  352.4 3.1 reduce_sum.86
  355.5 1.2 reshape.76
  356.7 46.2 %all-to-all-done.4 = bf16[1,4,160,3584]{3,2,0,1:T(8,128)(2,1)} async-done(((bf16[1,4,160,3584]{3,2,0,1:T(8,128)(2,1)}), bf16[1,4,160,3584]{3,2,0,1:T(8,128)(2,1)}, u32[]{:S(2)}, u32[]{:S(2)}) %all-to-all-start.4) | async-done | bytes 4587552 | tf_op jit(solution)/shard_map/all_to_all | solution.py:59
  402.9 6.0 %all-to-all-start.2 = ((bf16[1,8,20,3584]{3,2,0,1:T(8,128)(2,1)}), bf16[1,8,20,3584]{3,2,0,1:T(8,128)(2,1)S(1)}, u32[]{:S(2)}, u32[]{:S(2)}) async-start(bf16[1,8,20,3584]{3,2,0,1:T(8,128)(2,1)} %bitcast.72), calls=%async_computation.2 | async-start | bytes 2752512 | tf_op jit(solution)/shard_map/all_to_all | solution.py:62
  408.9 4.3 reduce_sum.91
  413.2 2.3 reshape.77
  415.4 28.6 %all-to-all-done.2 = bf16[1,8,20,3584]{3,2,0,1:T(8,128)(2,1)S(1)} async-done(((bf16[1,8,20,3584]{3,2,0,1:T(8,128)(2,1)}), bf16[1,8,20,3584]{3,2,0,1:T(8,128)(2,1)S(1)}, u32[]{:S(2)}, u32[]{:S(2)}) %all-to-all-start.2) | async-done | bytes 1146912 | tf_op jit(solution)/shard_map/all_to_all | solution.py:62
  444.0 1.1 copy-done.2
  445.1 3.6 all-to-all-start.5
  448.7 2.2 squeeze.30
  450.9 2.8 fusion.3
  453.7 3.6 collective-permute-start
  457.3 5.8 %convolution_bitcast_fusion.1 = f32[1,1,3584,256]{3,2,1,0:T(8,128)} fusion(bf16[640,3584]{1,0:T(8,128)(2,1)} %squeeze.34, bf16[640,256]{1,0:T(8,128)(2,1)S(1)} %fusion.15), kind=kOutput, calls=%fused_computation.5 | convolution fusion | flops 1174405120 | bytes 8585216 | tf_op jit(solution)/shard_map/dot_general | solution.py:82
  463.1 38.9 %all-to-all-done.5 = bf16[1,8,20,3584]{3,2,0,1:T(8,128)(2,1)S(1)} async-done(((bf16[1,8,20,3584]{3,2,0,1:T(8,128)(2,1)}), bf16[1,8,20,3584]{3,2,0,1:T(8,128)(2,1)S(1)}, u32[]{:S(2)}, u32[]{:S(2)}) %all-to-all-start.5) | async-done | bytes 1146912 | tf_op jit(solution)/shard_map/all_to_all | solution.py:62
  501.9 1.1 squeeze.35
  503.1 2.0 fusion.2
  505.1 4.8 collective-permute-start.1
  510.0 5.8 %convolution_bitcast_fusion = f32[1,1,256,3584]{3,2,1,0:T(8,128)} fusion(bf16[640,3584]{1,0:T(8,128)(2,1)} %squeeze.33, f32[640,256]{1,0:T(8,128)S(1)} %copy-done.4), kind=kOutput, calls=%fused_computation.4 | convolution fusion | flops 1175224320 | bytes 8912896 | tf_op jit(solution)/shard_map/dot_general | solution.py:85
  515.7 15.2 %collective-permute-done.1 = bf16[1,64,3584]{2,1,0:T(8,128)(2,1)S(1)} collective-permute-done((bf16[1,64,3584]{2,1,0:T(8,128)(2,1)S(1)}, bf16[1,64,3584]{2,1,0:T(8,128)(2,1)S(1)}, u32[]{:S(2)}, u32[]{:S(2)}) %collective-permute-start.1) | collective-permute-done | bytes 458784 | tf_op jit(solution)/shard_map/ppermute | solution.py:13
  530.9 1.8 copy.77
  532.7 0.8 copy.78
  (26 shorter events, 0.2 us)
Async XLA Ops:
  7.2 143.4 %copy-start = (bf16[1,1,3584,256]{3,2,1,0:T(8,128)(2,1)S(1)}, bf16[1,1,3584,256]{3,2,1,0:T(8,128)(2,1)}, u32[]{:S(2)}) copy-start(bf16[1,1,3584,256]{3,2,1,0:T(8,128)(2,1)} %param.16) | copy-start | bytes 5505028
  7.2 128.7 %all-gather.3.cloned.1.call-start = ((), (), s32[]{:S(2)}) async-start(), calls=%async_computation.6 | async-start | bytes 5734400 | tf_op jit(solution)/shard_map/all_gather | solution.py:52
  56.1 1.4 copy-start.8
  56.1 2.3 copy-start.9
  56.1 3.1 copy-start.7
  57.5 220.3 %all-gather.5.cloned.1.call-start = ((), (), s32[]{:S(2)}) async-start(), calls=%async_computation.7 | async-start | bytes 11468800 | tf_op jit(solution)/shard_map/all_gather | solution.py:52
  58.5 0.6 copy-start.5
  161.2 186.3 %all-to-all-start.1 = ((bf16[1,4,160,3584]{3,2,0,1:T(8,128)(2,1)}), bf16[1,4,160,3584]{3,2,0,1:T(8,128)(2,1)}, u32[]{:S(2)}, u32[]{:S(2)}) async-start(bf16[1,4,160,3584]{3,2,0,1:T(8,128)(2,1)} %bitcast.74), calls=%async_computation.1 | async-start | bytes 9175040 | tf_op jit(solution)/shard_map/all_to_all | solution.py:59
  337.9 4.7 copy-start.1
  337.9 4.7 copy-start.10
  341.7 0.9 copy-start.3
  347.5 55.4 %all-to-all-start.4 = ((bf16[1,4,160,3584]{3,2,0,1:T(8,128)(2,1)}), bf16[1,4,160,3584]{3,2,0,1:T(8,128)(2,1)}, u32[]{:S(2)}, u32[]{:S(2)}) async-start(bf16[1,4,160,3584]{3,2,0,1:T(8,128)(2,1)} %bitcast.71), calls=%async_computation.4 | async-start | bytes 9175040 | tf_op jit(solution)/shard_map/all_to_all | solution.py:59
  402.9 41.1 %all-to-all-start.2 = ((bf16[1,8,20,3584]{3,2,0,1:T(8,128)(2,1)}), bf16[1,8,20,3584]{3,2,0,1:T(8,128)(2,1)S(1)}, u32[]{:S(2)}, u32[]{:S(2)}) async-start(bf16[1,8,20,3584]{3,2,0,1:T(8,128)(2,1)} %bitcast.72), calls=%async_computation.2 | async-start | bytes 2752512 | tf_op jit(solution)/shard_map/all_to_all | solution.py:62
  444.0 1.1 copy-start.2
  445.1 56.8 %all-to-all-start.5 = ((bf16[1,8,20,3584]{3,2,0,1:T(8,128)(2,1)}), bf16[1,8,20,3584]{3,2,0,1:T(8,128)(2,1)S(1)}, u32[]{:S(2)}, u32[]{:S(2)}) async-start(bf16[1,8,20,3584]{3,2,0,1:T(8,128)(2,1)} %bitcast.16), calls=%async_computation.5 | async-start | bytes 2752512 | tf_op jit(solution)/shard_map/all_to_all | solution.py:62
  453.7 62.1 %collective-permute-start = (bf16[1,64,3584]{2,1,0:T(8,128)(2,1)}, bf16[1,64,3584]{2,1,0:T(8,128)(2,1)}, u32[]{:S(2)}, u32[]{:S(2)}) collective-permute-start(bf16[1,64,3584]{2,1,0:T(8,128)(2,1)} %fusion.3), channel_id=1, source_target_pairs={{0,32},{32,64},{64,96},{96,128},{128,160},{160,192},{192,224},{224... | collective-permute-start | bytes 1376264 | tf_op jit(solution)/shard_map/ppermute | solution.py:13
  463.1 40.0 %copy-start.6 = (f32[64,160]{1,0:T(8,128)S(1)}, f32[64,160]{1,0:T(8,128)}, u32[]{:S(2)}) copy-start(f32[64,160]{1,0:T(8,128)} %copy-done.5) | copy-start | bytes 122884
  503.1 6.9 %copy-start.4 = (f32[640,256]{1,0:T(8,128)S(1)}, f32[640,256]{1,0:T(8,128)}, u32[]{:S(2)}) copy-start(f32[640,256]{1,0:T(8,128)} %copy-done.3) | copy-start | bytes 1966084
  505.1 25.8 %collective-permute-start.1 = (bf16[1,64,3584]{2,1,0:T(8,128)(2,1)S(1)}, bf16[1,64,3584]{2,1,0:T(8,128)(2,1)S(1)}, u32[]{:S(2)}, u32[]{:S(2)}) collective-permute-start(bf16[1,64,3584]{2,1,0:T(8,128)(2,1)S(1)} %fusion.2), channel_id=1, source_target_pairs={{0,224},{32,0},{64,32},{96,64},{128,96},{160,128},{192,160},{224,1... | collective-permute-start | bytes 1376264 | tf_op jit(solution)/shard_map/ppermute | solution.py:13
Sparse Core Ops, SparseCore 0:
  57.6 78.2 all-gather.2
  137.7 140.0 all-gather.4
where the time goes:
time: 542 us; the launch traced here: 540 us
  waiting for transfers between devices  252 us (46%)
  local copies, waits for them, and re-layouts  97.2 us (18%)
  blocking collectives  93.4 us (17%)
  matrix products  42.9 us (8%)
  starting transfers between devices  28.2 us (5%)
  between operations  14.2 us (3%)
  other arithmetic  12.1 us (2%)
    all_gather x2, waiting for transfers between devices, send_rows(): gathered = lax.all_gather(received, 'em', axis=1, tiled=True)  123 us
    all_to_all x2, blocking collectives, send_rows(): lax.all_to_all(chunks, 'eg', split_axis=1, concat_axis=1, tiled=True)  93.4 us
    all_to_all x2, waiting for transfers between devices, send_back(): back = lax.all_to_all(summed, 'eg', split_axis=1, concat_axis=1, tiled=True)  67.4 us
    all_to_all x2, waiting for transfers between devices, send_back(): lax.all_to_all(arranged, 'em', split_axis=1, concat_axis=1, tiled=True)  46.2 us
    slice x1, local copies, waits for them, and re-layouts, local(): got_b[0]  45.6 us
    ppermute x2, waiting for transfers between devices, passed_along(): return lax.ppermute(value, axis, pairs)  15.2 us
  transfers between devices with their start and end apart: 8, of which 6 were waited for; matrix products, arithmetic and copies ran while one was open for 26% of the time, Pallas kernels for 0%

commit v1 on v0

--- a/solution.py
+++ b/solution.py
@@ -48,7 +48,9 @@
 def send_rows(stacked, experts, slot_cap):
     count, _, model_width = stacked.shape
     chunks = stacked.reshape(count, experts, slot_cap, model_width)
-    received = lax.all_to_all(chunks, "eg", split_axis=1, concat_axis=1, tiled=True)
+    pieces = jnp.split(chunks, lax.axis_size("eg"), axis=1)
+    incoming = lax.all_to_all(jnp.stack(pieces), "eg", 0, 0)
+    received = jnp.concatenate(incoming, axis=1)
     gathered = lax.all_gather(received, "em", axis=1, tiled=True)
     return gathered.reshape(count, -1, model_width)
 

time: 542 us -> 548 us (1.011)
  blocking collectives: 93.4 us -> 55.2 us
  local copies, waits for them, and re-layouts: 97.2 us -> 124 us
  waiting for transfers between devices: 252 us -> 264 us
  starting transfers between devices: 28.2 us -> 36 us
    all_to_all x2 -> x1, blocking collectives: 93.4 us -> 55.2 us  [send_rows(): incoming = lax.all_to_all(jnp.stack(pieces), 'eg', 0, 0)]
    unnamed x26 -> x41, local copies, waits for them, and re-layouts: 6.15 us -> 25.6 us
    all_to_all x0 -> x1, waiting for transfers between devices: none -> 11.1 us  [send_rows(): incoming = lax.all_to_all(jnp.stack(pieces), 'eg', 0, 0)]
    all_to_all x0 -> x1, starting transfers between devices: none -> 7.73 us  [send_rows(): incoming = lax.all_to_all(jnp.stack(pieces), 'eg', 0, 0)]
    another operation x0 -> x3, local copies, waits for them, and re-layouts: none -> 5.95 us  [send_rows(): incoming = lax.all_to_all(jnp.stack(pieces), 'eg', 0, 0)]
  transfers between devices with their start and end apart: 8 -> 9, of which waited for: 6 -> 7; matrix products, arithmetic and copies ran while one was open for 26% -> 29% of each run, Pallas kernels for 0% -> 0%
where the time goes in v1:
time: 548 us; the launch traced here: 546 us
  waiting for transfers between devices  264 us (48%)
  local copies, waits for them, and re-layouts  124 us (23%)
  blocking collectives  55.2 us (10%)
  matrix products  42.9 us (8%)
  starting transfers between devices  36 us (7%)
  between operations  14.2 us (3%)
  other arithmetic  10.5 us (2%)
    all_gather x2, waiting for transfers between devices, send_rows(): gathered = lax.all_gather(received, 'em', axis=1, tiled=True)  124 us
    all_to_all x2, waiting for transfers between devices, send_back(): back = lax.all_to_all(summed, 'eg', split_axis=1, concat_axis=1, tiled=True)  67.4 us
    all_to_all x1, blocking collectives, send_rows(): incoming = lax.all_to_all(jnp.stack(pieces), 'eg', 0, 0)  55.2 us
    all_to_all x2, waiting for transfers between devices, send_back(): lax.all_to_all(arranged, 'em', split_axis=1, concat_axis=1, tiled=True)  46.2 us
    slice x1, local copies, waits for them, and re-layouts, local(): got_b[0]  45.6 us
    unnamed x41, local copies, waits for them, and re-layouts  25.6 us
    ppermute x2, waiting for transfers between devices, passed_along(): return lax.ppermute(value, axis, pairs)  15.2 us
    all_to_all x1, waiting for transfers between devices, send_rows(): incoming = lax.all_to_all(jnp.stack(pieces), 'eg', 0, 0)  11.1 us
  transfers between devices with their start and end apart: 9, of which 7 were waited for; matrix products, arithmetic and copies ran while one was open for 29% of the time, Pallas kernels for 0%

profile of v1, /device:TPU:1, one launch (start us, length us, event | category | flops | bytes accessed | tf_op | source)
XLA Modules:
  0.0 546.0 jit_solution(216900043006331128)
XLA Ops:
  7.2 0.9 copy.65
  8.9 0.7 bitcast_add_fusion.1
  9.6 1.4 convert_reduce_fusion.1
  11.0 2.5 convolution_convert_fusion.4
  13.5 1.4 reshape_broadcast_in_dim.9
  14.9 0.7 fusion.42
  16.9 0.7 fusion.39
  17.6 0.7 fusion.38
  18.3 0.7 fusion.37
  19.0 0.7 fusion.36
  20.3 7.7 %all-to-all-start = ((bf16[8,1,1,20,3584]{4,3,2,1,0:T(8,128)(2,1)}), bf16[8,1,1,20,3584]{4,3,2,1,0:T(8,128)(2,1)S(1)}, u32[]{:S(2)}, u32[]{:S(2)}) async-start(bf16[8,1,1,20,3584]{4,3,2,1,0:T(8,128)(2,1)} %fusion.35), calls=%async_computation | async-start | bytes 2752512 | tf_op jit(solution)/shard_map/all_to_all | solution.py:52
  29.7 2.5 convolution_convert_fusion.3
  32.2 2.3 stack.72
  34.5 2.6 constant_dynamic-update-slice_fusion.1
  37.1 2.1 convolution_convert_fusion.2
  39.2 2.3 stack.73
  41.4 2.5 constant_dynamic-update-slice_fusion
  43.9 1.7 fusion.32
  45.7 1.7 fusion.31
  47.4 1.7 fusion.30
  49.1 1.7 fusion.29
  50.9 11.1 %all-to-all-done = bf16[8,1,1,20,3584]{4,3,2,1,0:T(8,128)(2,1)S(1)} async-done(((bf16[8,1,1,20,3584]{4,3,2,1,0:T(8,128)(2,1)}), bf16[8,1,1,20,3584]{4,3,2,1,0:T(8,128)(2,1)S(1)}, u32[]{:S(2)}, u32[]{:S(2)}) %all-to-all-start) | async-done | bytes 1146912 | tf_op jit(solution)/shard_map/all_to_all | solution.py:52
  62.0 1.3 copy.67
  63.4 1.7 fusion.28
  65.1 1.7 fusion.27
  66.9 1.7 fusion.26
  68.6 1.7 fusion.25
  70.3 3.5 copy.80
  73.9 55.2 %all_to_all.30 = bf16[8,2,1,20,3584]{4,1,3,2,0:T(2,128)(2,1)} all-to-all(bf16[8,2,1,20,3584]{4,1,3,2,0:T(2,128)(2,1)S(1)} %copy.80), channel_id=1, replica_groups=mesh['pipe'=8,'eg'=8,'em'=4] {'eg'}, dimensions={0} | all-to-all | bytes 4587520 | tf_op jit(solution)/shard_map/all_to_all | solution.py:52
  129.1 12.4 %all-gather.5.cloned.1.call-done = bf16[32,1,1,20,3584]{4,0,3,2,1:T(8,128)(2,1)} async-done(((bf16[8,1,1,20,3584]{4,0,3,2,1:T(8,128)(2,1)}), bf16[32,1,1,20,3584]{4,0,3,2,1:T(8,128)(2,1)}) %all-gather.5.cloned.1.call-update) | async-done | bytes 4587536 | tf_op jit(solution)/shard_map/all_gather | solution.py:54
  141.5 7.3 %copy.68 = bf16[32,1,1,20,3584]{4,3,0,2,1:T(8,128)(2,1)} copy(bf16[32,1,1,20,3584]{4,0,3,2,1:T(8,128)(2,1)} %all-gather.5.cloned.1.call-done) | data formatting | bytes 9175040 | tf_op jit(solution)/shard_map/all_gather | solution.py:54
  148.8 7.4 %squeeze_reshape.3 = bf16[640,3584]{1,0:T(8,128)(2,1)} reshape(bf16[32,1,1,20,3584]{4,3,0,2,1:T(8,128)(2,1)} %copy.68) | data formatting | bytes 9175040 | tf_op jit(solution)/shard_map/squeeze;reshape | solution.py:114
  156.2 10.6 %convolution_convert_fusion.1 = bf16[640,3584]{1,0:T(8,128)(2,1)} fusion(bf16[1,1,256,3584]{3,2,1,0:T(8,128)(2,1)} %param.17, bf16[640,3584]{1,0:T(8,128)(2,1)} %squeeze_reshape.3, bf16[1,1,3584,256]{3,2,1,0:T(8,128)(2,1)S(1)} %copy-done), kind=kOutput, calls=%fused_computation.3 | convolution fusion | flops 2351923200 | bytes 12845056 | tf_op jit(solution)/shard_map/dot_general | solution.py:71
  166.8 5.2 all-to-all-start.1
  172.1 111.3 %all-gather.7.cloned.1.call-done = bf16[2,32,1,20,3584]{4,0,3,2,1:T(2,128)(2,1)} async-done(((bf16[2,8,1,20,3584]{4,0,3,2,1:T(2,128)(2,1)}), bf16[2,32,1,20,3584]{4,0,3,2,1:T(2,128)(2,1)}) %all-gather.7.cloned.1.call-update) | async-done | bytes 9175056 | tf_op jit(solution)/shard_map/all_gather | solution.py:54
  283.4 45.6 %slice_reduce_fusion = (bf16[32,20,3584]{2,1,0:T(8,128)(2,1)}, bf16[32,20,3584]{2,1,0:T(8,128)(2,1)}) fusion(bf16[2,32,1,20,3584]{4,0,3,2,1:T(2,128)(2,1)} %all-gather.7.cloned.1.call-done), kind=kLoop, calls=%fused_computation | loop fusion | bytes 18350080 | tf_op jit(solution)/shard_map/slice | solution.py:117
  328.9 7.3 %squeeze.34 = bf16[640,3584]{1,0:T(8,128)(2,1)} reshape(bf16[32,20,3584]{2,1,0:T(8,128)(2,1)} %get-tuple-element.4) | data formatting | bytes 9175040 | tf_op jit(solution)/shard_map/squeeze | solution.py:117
  336.2 7.3 %squeeze.33 = bf16[640,3584]{1,0:T(8,128)(2,1)} reshape(bf16[32,20,3584]{2,1,0:T(8,128)(2,1)} %get-tuple-element.5) | data formatting | bytes 9175040 | tf_op jit(solution)/shard_map/squeeze | solution.py:117
  343.5 3.8 fusion.8
  347.3 0.8 copy-done.4
  348.1 1.4 fusion.15
  349.5 3.6 convolution_convert_fusion
  353.1 4.9 all-to-all-start.4
  358.0 3.1 reduce_sum.86
  361.1 1.2 reshape.86
  362.3 46.2 %all-to-all-done.4 = bf16[1,4,160,3584]{3,2,0,1:T(8,128)(2,1)} async-done(((bf16[1,4,160,3584]{3,2,0,1:T(8,128)(2,1)}), bf16[1,4,160,3584]{3,2,0,1:T(8,128)(2,1)}, u32[]{:S(2)}, u32[]{:S(2)}) %all-to-all-start.4) | async-done | bytes 4587552 | tf_op jit(solution)/shard_map/all_to_all | solution.py:61
  408.5 6.0 %all-to-all-start.2 = ((bf16[1,8,20,3584]{3,2,0,1:T(8,128)(2,1)}), bf16[1,8,20,3584]{3,2,0,1:T(8,128)(2,1)S(1)}, u32[]{:S(2)}, u32[]{:S(2)}) async-start(bf16[1,8,20,3584]{3,2,0,1:T(8,128)(2,1)} %bitcast.153), calls=%async_computation.2 | async-start | bytes 2752512 | tf_op jit(solution)/shard_map/all_to_all | solution.py:64
  414.5 4.3 reduce_sum.91
  418.8 2.3 reshape.89
  421.1 28.6 %all-to-all-done.2 = bf16[1,8,20,3584]{3,2,0,1:T(8,128)(2,1)S(1)} async-done(((bf16[1,8,20,3584]{3,2,0,1:T(8,128)(2,1)}), bf16[1,8,20,3584]{3,2,0,1:T(8,128)(2,1)S(1)}, u32[]{:S(2)}, u32[]{:S(2)}) %all-to-all-start.2) | async-done | bytes 1146912 | tf_op jit(solution)/shard_map/all_to_all | solution.py:64
  449.6 1.1 copy-done.2
  450.7 3.6 all-to-all-start.5
  454.3 2.2 squeeze.30
  456.5 2.8 fusion.3
  459.3 3.6 collective-permute-start
  462.9 5.8 %convolution_bitcast_fusion.1 = f32[1,1,3584,256]{3,2,1,0:T(8,128)} fusion(bf16[640,3584]{1,0:T(8,128)(2,1)} %squeeze.34, bf16[640,256]{1,0:T(8,128)(2,1)S(1)} %fusion.15), kind=kOutput, calls=%fused_computation.5 | convolution fusion | flops 1174405120 | bytes 8585216 | tf_op jit(solution)/shard_map/dot_general | solution.py:84
  468.7 38.9 %all-to-all-done.5 = bf16[1,8,20,3584]{3,2,0,1:T(8,128)(2,1)S(1)} async-done(((bf16[1,8,20,3584]{3,2,0,1:T(8,128)(2,1)}), bf16[1,8,20,3584]{3,2,0,1:T(8,128)(2,1)S(1)}, u32[]{:S(2)}, u32[]{:S(2)}) %all-to-all-start.5) | async-done | bytes 1146912 | tf_op jit(solution)/shard_map/all_to_all | solution.py:64
  507.6 1.1 squeeze.35
  508.7 2.0 fusion.2
  510.7 4.8 collective-permute-start.1
  515.6 5.8 %convolution_bitcast_fusion = f32[1,1,256,3584]{3,2,1,0:T(8,128)} fusion(bf16[640,3584]{1,0:T(8,128)(2,1)} %squeeze.33, f32[640,256]{1,0:T(8,128)S(1)} %copy-done.5), kind=kOutput, calls=%fused_computation.4 | convolution fusion | flops 1175224320 | bytes 8912896 | tf_op jit(solution)/shard_map/dot_general | solution.py:87
  521.3 15.2 %collective-permute-done.1 = bf16[1,64,3584]{2,1,0:T(8,128)(2,1)S(1)} collective-permute-done((bf16[1,64,3584]{2,1,0:T(8,128)(2,1)S(1)}, bf16[1,64,3584]{2,1,0:T(8,128)(2,1)S(1)}, u32[]{:S(2)}, u32[]{:S(2)}) %collective-permute-start.1) | collective-permute-done | bytes 458784 | tf_op jit(solution)/shard_map/ppermute | solution.py:13
  536.6 1.8 copy.109
  538.4 0.8 copy.110
  (44 shorter events, 4.6 us)
Async XLA Ops:
  7.2 149.0 %copy-start = (bf16[1,1,3584,256]{3,2,1,0:T(8,128)(2,1)S(1)}, bf16[1,1,3584,256]{3,2,1,0:T(8,128)(2,1)}, u32[]{:S(2)}) copy-start(bf16[1,1,3584,256]{3,2,1,0:T(8,128)(2,1)} %param.16) | copy-start | bytes 5505028
  16.9 11.2 %copy-start.8 = (s32[1,64,2]{1,2,0:T(2,128)S(1)}, s32[1,64,2]{1,2,0:T(2,128)}, u32[]{:S(2)}) copy-start(s32[1,64,2]{1,2,0:T(2,128)} %param.13) | copy-start | bytes 1540
  17.6 11.4 %copy-start.9 = (f32[1,64,2]{1,2,0:T(2,128)S(1)}, f32[1,64,2]{1,2,0:T(2,128)}, u32[]{:S(2)}) copy-start(f32[1,64,2]{1,2,0:T(2,128)} %param.14) | copy-start | bytes 1540
  20.3 41.7 %all-to-all-start = ((bf16[8,1,1,20,3584]{4,3,2,1,0:T(8,128)(2,1)}), bf16[8,1,1,20,3584]{4,3,2,1,0:T(8,128)(2,1)S(1)}, u32[]{:S(2)}, u32[]{:S(2)}) async-start(bf16[8,1,1,20,3584]{4,3,2,1,0:T(8,128)(2,1)} %fusion.35), calls=%async_computation | async-start | bytes 2752512 | tf_op jit(solution)/shard_map/all_to_all | solution.py:52
  28.0 113.5 %all-gather.5.cloned.1.call-start = ((), (), s32[]{:S(2)}) async-start(), calls=%async_computation.6 | async-start | bytes 5734400 | tf_op jit(solution)/shard_map/all_gather | solution.py:54
  29.1 0.6 copy-start.6
  34.5 2.6 copy-start.3
  63.3 220.0 %all-gather.7.cloned.1.call-start = ((), (), s32[]{:S(2)}) async-start(), calls=%async_computation.7 | async-start | bytes 11468800 | tf_op jit(solution)/shard_map/all_gather | solution.py:54
  166.8 186.3 %all-to-all-start.1 = ((bf16[1,4,160,3584]{3,2,0,1:T(8,128)(2,1)}), bf16[1,4,160,3584]{3,2,0,1:T(8,128)(2,1)}, u32[]{:S(2)}, u32[]{:S(2)}) async-start(bf16[1,4,160,3584]{3,2,0,1:T(8,128)(2,1)} %bitcast.154), calls=%async_computation.1 | async-start | bytes 9175040 | tf_op jit(solution)/shard_map/all_to_all | solution.py:61
  343.5 4.7 copy-start.1
  343.5 4.7 copy-start.10
  347.3 0.9 copy-start.4
  353.1 55.4 %all-to-all-start.4 = ((bf16[1,4,160,3584]{3,2,0,1:T(8,128)(2,1)}), bf16[1,4,160,3584]{3,2,0,1:T(8,128)(2,1)}, u32[]{:S(2)}, u32[]{:S(2)}) async-start(bf16[1,4,160,3584]{3,2,0,1:T(8,128)(2,1)} %bitcast.151), calls=%async_computation.4 | async-start | bytes 9175040 | tf_op jit(solution)/shard_map/all_to_all | solution.py:61
  408.5 41.1 %all-to-all-start.2 = ((bf16[1,8,20,3584]{3,2,0,1:T(8,128)(2,1)}), bf16[1,8,20,3584]{3,2,0,1:T(8,128)(2,1)S(1)}, u32[]{:S(2)}, u32[]{:S(2)}) async-start(bf16[1,8,20,3584]{3,2,0,1:T(8,128)(2,1)} %bitcast.153), calls=%async_computation.2 | async-start | bytes 2752512 | tf_op jit(solution)/shard_map/all_to_all | solution.py:64
  449.6 1.1 copy-start.2
  450.7 56.8 %all-to-all-start.5 = ((bf16[1,8,20,3584]{3,2,0,1:T(8,128)(2,1)}), bf16[1,8,20,3584]{3,2,0,1:T(8,128)(2,1)S(1)}, u32[]{:S(2)}, u32[]{:S(2)}) async-start(bf16[1,8,20,3584]{3,2,0,1:T(8,128)(2,1)} %bitcast.32), calls=%async_computation.5 | async-start | bytes 2752512 | tf_op jit(solution)/shard_map/all_to_all | solution.py:64
  459.3 62.0 %collective-permute-start = (bf16[1,64,3584]{2,1,0:T(8,128)(2,1)}, bf16[1,64,3584]{2,1,0:T(8,128)(2,1)}, u32[]{:S(2)}, u32[]{:S(2)}) collective-permute-start(bf16[1,64,3584]{2,1,0:T(8,128)(2,1)} %fusion.3), channel_id=1, source_target_pairs={{0,32},{32,64},{64,96},{96,128},{128,160},{160,192},{192,224},{224... | collective-permute-start | bytes 1376264 | tf_op jit(solution)/shard_map/ppermute | solution.py:13
  468.7 40.0 %copy-start.7 = (f32[64,160]{1,0:T(8,128)S(1)}, f32[64,160]{1,0:T(8,128)}, u32[]{:S(2)}) copy-start(f32[64,160]{1,0:T(8,128)} %copy-done.6) | copy-start | bytes 122884
  508.7 6.9 %copy-start.5 = (f32[640,256]{1,0:T(8,128)S(1)}, f32[640,256]{1,0:T(8,128)}, u32[]{:S(2)}) copy-start(f32[640,256]{1,0:T(8,128)} %copy-done.4) | copy-start | bytes 1966084
  510.7 25.8 %collective-permute-start.1 = (bf16[1,64,3584]{2,1,0:T(8,128)(2,1)S(1)}, bf16[1,64,3584]{2,1,0:T(8,128)(2,1)S(1)}, u32[]{:S(2)}, u32[]{:S(2)}) collective-permute-start(bf16[1,64,3584]{2,1,0:T(8,128)(2,1)S(1)} %fusion.2), channel_id=1, source_target_pairs={{0,224},{32,0},{64,32},{96,64},{128,96},{160,128},{192,160},{224,1... | collective-permute-start | bytes 1376264 | tf_op jit(solution)/shard_map/ppermute | solution.py:13
Sparse Core Ops, SparseCore 0:
  63.5 77.9 all-gather.4
  143.3 140.0 all-gather.6
